TPU v7x, 32 devices: a whole 2x2x4 slice. The times are simulated.
32 devices in a mesh: dp: 4 (over y, x), expert: 8 (over z, core).
Axes of the slice: x: 2, y: 2, z: 4, core: 2. Of those that a mesh axis runs over, the one named last changes fastest.
Arguments:
- tokens: bfloat16 [4096, 2048], P(('dp', 'expert')), may hold values from -6 to 6
- expert_ids: int32 [4096, 4], P(('dp', 'expert')), may hold values from 0 to 7, all different within a row; in each aligned block of 128 rows (0 to 127, 128 to 255, ...) at most 80 rows name the same one
- probs: float32 [4096, 4], P(('dp', 'expert')), may hold values from 0.2 to 1
- trade: int32 [4], replicated, may hold values from 0 to 1, as said below
- gate_weight: bfloat16 [8, 2048, 768], P('expert'), may hold values from -0.125 to 0.125
- up_weight: bfloat16 [8, 2048, 768], P('expert'), may hold values from -0.125 to 0.125
- down_weight: bfloat16 [8, 768, 2048], P('expert'), may hold values from -0.21875 to 0.21875
- out_grad: bfloat16 [4096, 2048], P(('dp', 'expert')), may hold values from -0.29882812 to 0.29882812
Outputs:
- combined: bfloat16 [4096, 2048], P(('dp', 'expert'))
- gate_grad: bfloat16 [8, 2048, 768], P('expert', 'dp')
- up_grad: bfloat16 [8, 2048, 768], P('expert', 'dp')
- down_grad: bfloat16 [8, 768, 2048], P('expert', None, 'dp')
Inputs may be any that keep to these rules, and one draw needn't show every extreme that they name: `trade`: index k below 4 pairs expert index k with k + 4; at least one pair trades and at least one does not. `expert_ids`: each row names 4 different experts. Within the 128 rows of one device no expert is named by more than 80 rows, a bound that some block reaches.
All inputs are finite; a program needn't handle non-finite values.
Results may differ from a plain program's by a relative error of at most 0.0095.
Values may be sent and summed in bfloat16 or wider, within the bound.
A program may use at most 128 MiB of HBM per device.

v0:
```python
import jax
import jax.numpy as jnp
from jax import lax
from jax.sharding import PartitionSpec as P


def local(tokens, expert_ids, probs, trade, gate_weight, up_weight, down_weight, out_grad):
    tok_count, model_width = tokens.shape
    top_count = expert_ids.shape[1]
    hidden_width = gate_weight.shape[2]
    experts = lax.axis_size("expert")
    capacity = 5 * tok_count * top_count // (4 * experts)
    halfway = experts // 2
    chosen = expert_ids.reshape(-1)
    numbers = jnp.arange(experts, dtype=jnp.int32)
    onehot = (chosen[:, None] == numbers[None, :]).astype(jnp.int32)
    earlier = jnp.cumsum(onehot, axis=0) - onehot
    slots = chosen * capacity + jnp.sum(earlier * onehot, axis=1)
    owners = jnp.where(trade[numbers % halfway] == 1, jnp.bitwise_xor(numbers, halfway), numbers)
    pair_tokens = jnp.arange(chosen.shape[0], dtype=jnp.int32) // top_count
    send_rows = (
        jnp.zeros((experts * capacity, model_width), jnp.bfloat16)
        .at[slots]
        .set(tokens[pair_tokens])
    )
    send_rows = send_rows.reshape(experts, capacity, model_width)
    out_pairs = (probs[:, :, None] * out_grad[:, None, :].astype(jnp.float32)).astype(jnp.bfloat16)
    send_grads = (
        jnp.zeros((experts * capacity, model_width), jnp.bfloat16)
        .at[slots]
        .set(out_pairs.reshape(-1, model_width))
    )
    send_grads = send_grads.reshape(experts, capacity, model_width)
    send_rows = send_rows[owners]
    send_grads = send_grads[owners]
    w_gate = gate_weight[0]
    w_up = up_weight[0]
    w_down = down_weight[0]
    arrived = lax.all_to_all(send_rows, "expert", split_axis=0, concat_axis=0, tiled=True)
    lead = arrived.shape[:2]
    flat_rows = arrived.reshape(-1, model_width)
    gate_act = jnp.dot(flat_rows, w_gate, preferred_element_type=jnp.float32)
    up_act = jnp.dot(flat_rows, w_up, preferred_element_type=jnp.float32)
    forward_hidden = (gate_act * jax.nn.sigmoid(gate_act) * up_act).astype(jnp.bfloat16)
    expert_out = jnp.dot(forward_hidden, w_down, preferred_element_type=jnp.float32).astype(
        jnp.bfloat16
    )
    arrived, expert_out, hidden, gate_act, up_act = (
        arrived,
        expert_out.reshape(lead + (model_width,)),
        forward_hidden.reshape(lead + (hidden_width,)),
        gate_act.reshape(lead + (hidden_width,)),
        up_act.reshape(lead + (hidden_width,)),
    )
    returned = lax.all_to_all(expert_out, "expert", split_axis=0, concat_axis=0, tiled=True)
    out_rows = lax.all_to_all(send_grads, "expert", split_axis=0, concat_axis=0, tiled=True)
    returned = returned[owners]
    picked = returned.reshape(-1, model_width)[slots].reshape(tok_count, top_count, model_width)
    combined = jnp.sum(probs[:, :, None] * picked.astype(jnp.float32), axis=1).astype(jnp.bfloat16)
    expert_rows = arrived.reshape(-1, model_width)
    out_rows = out_rows.reshape(-1, model_width)
    hidden = hidden.reshape(-1, hidden_width)
    gate_act = gate_act.reshape(-1, hidden_width)
    up_act = up_act.reshape(-1, hidden_width)
    hidden_grad = lax.dot_general(
        out_rows, w_down, (((1,), (1,)), ((), ())), preferred_element_type=jnp.float32
    )
    sigma = jax.nn.sigmoid(gate_act)
    gate_back = (hidden_grad * up_act * (sigma * (1.0 + gate_act * (1.0 - sigma)))).astype(
        jnp.bfloat16
    )
    up_back = (hidden_grad * (gate_act * sigma)).astype(jnp.bfloat16)
    both_back = jnp.concatenate([gate_back, up_back], axis=1)
    first = lax.dot_general(
        expert_rows, both_back, (((0,), (0,)), ((), ())), preferred_element_type=jnp.float32
    )
    second = lax.dot_general(
        out_rows, hidden, (((0,), (0,)), ((), ())), preferred_element_type=jnp.float32
    )
    summed = lax.psum_scatter(
        jnp.concatenate([first, second], axis=1).astype(jnp.bfloat16),
        "dp",
        scatter_dimension=0,
        tiled=True,
    )
    gate_part = summed[:, :hidden_width]
    up_part = summed[:, hidden_width : 2 * hidden_width]
    down_part = summed[:, 2 * hidden_width :].T
    return (combined, gate_part[None], up_part[None], down_part[None])


def solution(mesh):
    return jax.shard_map(
        local,
        mesh=mesh,
        in_specs=(
            P(("dp", "expert"), None),
            P(("dp", "expert"), None),
            P(("dp", "expert"), None),
            P(),
            P("expert", None, None),
            P("expert", None, None),
            P("expert", None, None),
            P(("dp", "expert"), None),
        ),
        out_specs=(
            P(("dp", "expert"), None),
            P("expert", "dp", None),
            P("expert", "dp", None),
            P("expert", None, "dp"),
        ),
        check_vma=False,
    )
```

profile of v0, /device:TPU:0, one launch (start us, length us, event | category | flops | bytes accessed | tf_op | source)
XLA Modules:
  0.0 306.3 jit_solution(1818600435263554823)
XLA Ops:
  7.2 0.0 copy-start
  7.2 0.8 broadcast_multiply_fusion
  8.0 0.9 copy.17
  8.9 0.1 eq.44
  9.0 0.1 eq.40
  9.1 0.1 copy.16
  9.3 0.1 mul.70
  9.4 1.1 reduce-window.6
  10.5 0.2 slice_reduce_fusion
  10.8 4.2 %mul.77 = f32[128,4,2048]{2,1,0:T(4,128)} broadcast(bf16[128,2048]{1,0:T(8,128)(2,1)} %param.15), dimensions={0,2} | broadcast | bytes 4718592 | tf_op jit(solution)/shard_map/mul | solution.py:27
  15.0 0.0 copy-start.2
  15.0 0.0 copy-start.1
  15.0 5.3 %mul.78 = f32[512,2048]{1,0:T(8,128)} reshape(f32[128,4,2048]{2,1,0:T(4,128)} %mul.77) | data formatting | bytes 8388608 | tf_op jit(solution)/shard_map/mul | solution.py:27
  20.3 0.0 copy-done.2
  20.3 0.1 copy.15
  20.4 0.1 mul.75
  20.5 0.0 copy-done.1
  20.5 0.6 gather_fusion
  21.2 0.1 fusion.18
  21.3 7.1 %scatter_custom_fusion.1 = bf16[640,2048]{1,0:T(8,128)(2,1)} fusion(s32[512]{0:T(512)S(1)} %bitcast.59, f32[512,2048]{1,0:T(8,128)} %mul.78, f32[512]{0:T(512)S(1)} %mul.75, bf16[]{:T(256)} %constant.41.clone.1), kind=kCustom, calls=%fused_computation.21 | custom fusion | flops 2097152 | bytes 6817794 | tf_op jit(solution)/shard_map/scatter | solution.py:31
  28.4 4.0 %gather_fusion.4 = bf16[8,80,2048]{2,1,0:T(8,128)(2,1)} fusion(bf16[8,80,2048]{2,1,0:T(8,128)(2,1)} %bitcast.56, s32[1024]{0:T(1024)S(1)} %pad_clamp_fusion.1), kind=kCustom, calls=%fused_computation.5 | custom fusion | bytes 5242912 | tf_op jit(solution)/shard_map/gather | solution.py:35
  32.4 6.9 %all-to-all-start.2 = ((bf16[8,80,2048]{2,1,0:T(8,128)(2,1)}), bf16[8,80,2048]{2,1,0:T(8,128)(2,1)}, u32[]{:S(2)}, u32[]{:S(2)}) async-start(bf16[8,80,2048]{2,1,0:T(8,128)(2,1)} %gather_fusion.4), calls=%async_computation.2 | async-start | bytes 5242880 | tf_op jit(solution)/shard_map/all_to_all | solution.py:56
  39.3 11.7 %scatter_custom_fusion = bf16[640,2048]{1,0:T(8,128)(2,1)} fusion(s32[512]{0:T(512)S(1)} %bitcast.60, bf16[128,2048]{1,0:T(8,128)(2,1)} %param.8, s32[1024]{0:T(1024)S(1)} %pad_clamp_fusion.3, bf16[]{:T(256)} %constant.41.clone.1), kind=kCustom, calls=%fused_computation.22 | custom fusion | bytes 2621952 | tf_op jit(solution)/shard_map/scatter | solution.py:24
  51.1 4.0 %gather_fusion.1 = bf16[8,80,2048]{2,1,0:T(8,128)(2,1)} fusion(bf16[8,80,2048]{2,1,0:T(8,128)(2,1)} %bitcast.57, s32[1024]{0:T(1024)S(1)} %pad_clamp_fusion.1), kind=kCustom, calls=%fused_computation.2 | custom fusion | bytes 5242912 | tf_op jit(solution)/shard_map/gather | solution.py:34
  55.0 44.6 %all-to-all-done.2 = bf16[8,80,2048]{2,1,0:T(8,128)(2,1)} async-done(((bf16[8,80,2048]{2,1,0:T(8,128)(2,1)}), bf16[8,80,2048]{2,1,0:T(8,128)(2,1)}, u32[]{:S(2)}, u32[]{:S(2)}) %all-to-all-start.2) | async-done | bytes 2621472 | tf_op jit(solution)/shard_map/all_to_all | solution.py:56
  99.6 4.4 %all-to-all-start = ((bf16[8,80,2048]{2,1,0:T(8,128)(2,1)}), bf16[8,80,2048]{2,1,0:T(8,128)(2,1)}, u32[]{:S(2)}, u32[]{:S(2)}) async-start(bf16[8,80,2048]{2,1,0:T(8,128)(2,1)} %gather_fusion.1), calls=%async_computation | async-start | bytes 5242880 | tf_op jit(solution)/shard_map/all_to_all | solution.py:39
  104.0 0.2 reduce-scatter.2.cloned.1.call-start
  104.2 0.0 copy-done
  104.2 5.3 %fusion = f32[640,768]{1,0:T(8,128)} fusion(bf16[640,2048]{1,0:T(8,128)(2,1)} %bitcast.16, bf16[1,768,2048]{2,1,0:T(8,128)(2,1)S(1)} %copy-done), kind=kOutput, calls=%fused_computation.14 | convolution fusion | flops 2013265920 | bytes 7733248 | tf_op jit(solution)/shard_map/dot_general | solution.py:65
  109.6 54.7 %all-to-all-done = bf16[8,80,2048]{2,1,0:T(8,128)(2,1)} async-done(((bf16[8,80,2048]{2,1,0:T(8,128)(2,1)}), bf16[8,80,2048]{2,1,0:T(8,128)(2,1)}, u32[]{:S(2)}, u32[]{:S(2)}) %all-to-all-start) | async-done | bytes 2621472 | tf_op jit(solution)/shard_map/all_to_all | solution.py:39
  164.3 0.0 copy-start.3
  164.3 0.0 copy-start.4
  164.3 5.0 %fusion.3 = f32[640,768]{1,0:T(8,128)S(1)} fusion(bf16[640,2048]{1,0:T(8,128)(2,1)} %bitcast.9, bf16[1,2048,768]{2,1,0:T(8,128)(2,1)} %param.13), kind=kOutput, calls=%fused_computation.17 | convolution fusion | flops 2013265920 | bytes 7733248 | tf_op jit(solution)/shard_map/dot_general | solution.py:43
  169.3 0.0 copy-done.3
  169.3 0.0 copy-done.4
  169.3 4.6 %multiply_convert_fusion.3 = (bf16[640,768]{1,0:T(8,128)(2,1)S(1)}, bf16[640,768]{1,0:T(8,128)(2,1)S(1)}, bf16[640,768]{1,0:T(8,128)(2,1)S(1)}) fusion(f32[640,768]{1,0:T(8,128)S(1)} %copy-done.4, f32[640,768]{1,0:T(8,128)S(1)} %fusion.3, bf16[640,2048]{1,0:T(8,128)(2,1)} %bitcast.9, bf16[1,2048,768]{2,1,0:T(8,128)(2,1)S(1)} %copy-done.3), kind=kOutput, calls=%fused_computation.29 | convolution fusion | flops 2020638720 | bytes 12648448 | tf_op jit(solution)/shard_map/dot_general | solution.py:42
  173.9 0.0 copy-start.5
  174.0 5.0 %convolution_convert_fusion.1 = bf16[2048,768]{0,1:T(8,128)(2,1)S(1)} fusion(bf16[640,2048]{1,0:T(8,128)(2,1)} %bitcast.16, bf16[640,768]{1,0:T(8,128)(2,1)S(1)} %get-tuple-element.14), kind=kOutput, calls=%fused_computation.12 | convolution fusion | flops 2014838784 | bytes 6750208 | tf_op jit(solution)/shard_map/dot_general | solution.py:77
  178.9 0.0 copy-done.5
  178.9 7.1 %convolution_convert_fusion = bf16[2048,1536]{0,1:T(8,128)(2,1)S(1)} fusion(bf16[640,2048]{1,0:T(8,128)(2,1)} %bitcast.9, bf16[640,768]{1,0:T(8,128)(2,1)S(1)} %get-tuple-element.13, bf16[640,768]{1,0:T(8,128)(2,1)S(1)} %get-tuple-element.12), kind=kOutput, calls=%fused_computation.9 | convolution fusion | flops 4033609728 | bytes 10878976 | tf_op jit(solution)/shard_map/dot_general | solution.py:74
  186.1 11.5 %pad_maximum_fusion = bf16[2048,2304]{0,1:T(8,128)(2,1)} fusion(bf16[2048,768]{0,1:T(8,128)(2,1)S(1)} %convolution_convert_fusion.1, bf16[2048,1536]{0,1:T(8,128)(2,1)S(1)} %convolution_convert_fusion), kind=kLoop, calls=%fused_computation.8 | loop fusion | flops 18874368 | bytes 18874368 | tf_op jit(solution)/shard_map/concatenate | solution.py:81
  197.6 0.0 reduce-scatter.2.cloned.1.call-update
  197.6 4.9 %convolution_convert_fusion.2 = bf16[640,2048]{1,0:T(8,128)(2,1)} fusion(bf16[640,768]{1,0:T(8,128)(2,1)} %copy-done.5, bf16[1,768,2048]{2,1,0:T(8,128)(2,1)S(1)} %copy-done), kind=kOutput, calls=%fused_computation.13 | convolution fusion | flops 2014576640 | bytes 6750208 | tf_op jit(solution)/shard_map/dot_general | solution.py:45
  202.5 4.6 %all-to-all-start.1 = ((bf16[8,80,2048]{2,1,0:T(8,128)(2,1)}), bf16[8,80,2048]{2,1,0:T(8,128)(2,1)}, u32[]{:S(2)}, u32[]{:S(2)}) async-start(bf16[8,80,2048]{2,1,0:T(8,128)(2,1)} %bitcast.58), calls=%async_computation.1 | async-start | bytes 5242880 | tf_op jit(solution)/shard_map/all_to_all | solution.py:55
  207.2 60.3 %all-to-all-done.1 = bf16[8,80,2048]{2,1,0:T(8,128)(2,1)} async-done(((bf16[8,80,2048]{2,1,0:T(8,128)(2,1)}), bf16[8,80,2048]{2,1,0:T(8,128)(2,1)}, u32[]{:S(2)}, u32[]{:S(2)}) %all-to-all-start.1) | async-done | bytes 2621472 | tf_op jit(solution)/shard_map/all_to_all | solution.py:55
  267.4 3.9 %gather_fusion.2 = bf16[8,80,2048]{2,1,0:T(8,128)(2,1)} fusion(bf16[8,80,2048]{2,1,0:T(8,128)(2,1)} %all-to-all-done.1, s32[1024]{0:T(1024)S(1)} %pad_clamp_fusion.1), kind=kCustom, calls=%fused_computation.3 | custom fusion | bytes 5242912 | tf_op jit(solution)/shard_map/gather | solution.py:57
  271.3 7.4 %gather_fusion.3 = bf16[512,2048]{1,0:T(8,128)(2,1)} fusion(bf16[640,2048]{1,0:T(8,128)(2,1)} %bitcast.55, s32[1024]{0:T(1024)S(1)} %pad_clamp_fusion), kind=kCustom, calls=%fused_computation.4 | custom fusion | bytes 4196352 | tf_op jit(solution)/shard_map/gather | solution.py:58
  278.7 4.8 %reshape.194 = f32[128,4,2048]{2,1,0:T(4,128)} reshape(bf16[512,2048]{1,0:T(8,128)(2,1)} %gather_fusion.3) | data formatting | bytes 6291456 | tf_op jit(solution)/shard_map/convert_element_type | solution.py:59
  283.5 6.2 %multiply_reduce_fusion = bf16[128,2048]{1,0:T(8,128)(2,1)} fusion(f32[128,4,2048]{2,1,0:T(4,128)} %reshape.194, f32[128,4]{1,0:T(8,128)S(1)} %copy.15), kind=kLoop, calls=%fused_computation.11 | loop fusion | flops 1835008 | bytes 4720640 | tf_op jit(solution)/shard_map/reduce_sum | solution.py:59
  289.8 1.8 reduce-scatter.2.cloned.1.call-done
  291.6 3.1 slice_bitcast_fusion
  294.7 2.3 copy.20
  296.9 2.3 copy.21
  (11 shorter events, 0.1 us)
Async XLA Ops:
  7.2 97.1 %copy-start = (bf16[1,768,2048]{2,1,0:T(8,128)(2,1)S(1)}, bf16[1,768,2048]{2,1,0:T(8,128)(2,1)}, u32[]{:S(2)}) copy-start(bf16[1,768,2048]{2,1,0:T(8,128)(2,1)} %param.14) | copy-start | bytes 9437188
  15.0 5.3 %copy-start.2 = (f32[128,4]{0,1:T(4,128)S(1)}, f32[128,4]{0,1:T(4,128)}, u32[]{:S(2)}) copy-start(f32[128,4]{0,1:T(4,128)} %param.10) | copy-start | bytes 6148
  15.0 5.6 %copy-start.1 = (s32[4]{0:T(128)S(1)}, s32[4]{0:T(128)}, u32[]{:S(2)}) copy-start(s32[4]{0:T(128)} %param.11) | copy-start | bytes 52
  32.4 67.3 %all-to-all-start.2 = ((bf16[8,80,2048]{2,1,0:T(8,128)(2,1)}), bf16[8,80,2048]{2,1,0:T(8,128)(2,1)}, u32[]{:S(2)}, u32[]{:S(2)}) async-start(bf16[8,80,2048]{2,1,0:T(8,128)(2,1)} %gather_fusion.4), calls=%async_computation.2 | async-start | bytes 5242880 | tf_op jit(solution)/shard_map/all_to_all | solution.py:56
  99.6 64.7 %all-to-all-start = ((bf16[8,80,2048]{2,1,0:T(8,128)(2,1)}), bf16[8,80,2048]{2,1,0:T(8,128)(2,1)}, u32[]{:S(2)}, u32[]{:S(2)}) async-start(bf16[8,80,2048]{2,1,0:T(8,128)(2,1)} %gather_fusion.1), calls=%async_computation | async-start | bytes 5242880 | tf_op jit(solution)/shard_map/all_to_all | solution.py:39
  104.0 187.6 %reduce-scatter.2.cloned.1.call-start = ((), (), s32[]{:S(2)}) async-start(), calls=%async_computation.4 | async-start | bytes 11796480 | tf_op jit(solution)/shard_map/reduce_scatter | solution.py:80
  164.3 5.0 %copy-start.3 = (bf16[1,2048,768]{2,1,0:T(8,128)(2,1)S(1)}, bf16[1,2048,768]{2,1,0:T(8,128)(2,1)}, u32[]{:S(2)}) copy-start(bf16[1,2048,768]{2,1,0:T(8,128)(2,1)} %param.12) | copy-start | bytes 9437188
  164.3 5.0 %copy-start.4 = (f32[640,768]{1,0:T(8,128)S(1)}, f32[640,768]{1,0:T(8,128)}, u32[]{:S(2)}) copy-start(f32[640,768]{1,0:T(8,128)} %fusion) | copy-start | bytes 5898244
  173.9 5.0 %copy-start.5 = (bf16[640,768]{1,0:T(8,128)(2,1)}, bf16[640,768]{1,0:T(8,128)(2,1)S(1)}, u32[]{:S(2)}) copy-start(bf16[640,768]{1,0:T(8,128)(2,1)S(1)} %get-tuple-element.14) | copy-start | bytes 2949124
  202.5 64.9 %all-to-all-start.1 = ((bf16[8,80,2048]{2,1,0:T(8,128)(2,1)}), bf16[8,80,2048]{2,1,0:T(8,128)(2,1)}, u32[]{:S(2)}, u32[]{:S(2)}) async-start(bf16[8,80,2048]{2,1,0:T(8,128)(2,1)} %bitcast.58), calls=%async_computation.1 | async-start | bytes 5242880 | tf_op jit(solution)/shard_map/all_to_all | solution.py:55
Sparse Core Ops, SparseCore 0:
  197.8 93.8 reduce-scatter.1
where the time goes:
time: 312 us; the launch traced here: 306 us
  waiting for transfers between devices  161 us (52%)
  local copies, waits for them, and re-layouts  55.3 us (18%)
  matrix products  31.9 us (10%)
  other arithmetic  27 us (9%)
  starting transfers between devices  16.2 us (5%)
  between operations  14.5 us (5%)
    all_to_all x1, waiting for transfers between devices, local(): lax.all_to_all(expert_out, 'expert', split_axis=0, concat_axis=0, tiled=T...  60.3 us
    all_to_all x1, waiting for transfers between devices, local(): lax.all_to_all(send_rows, 'expert', split_axis=0, concat_axis=0, tiled=True)  54.7 us
    all_to_all x1, waiting for transfers between devices, local(): lax.all_to_all(send_grads, 'expert', split_axis=0, concat_axis=0, tiled=T...  44.6 us
    scatter x1, local copies, waits for them, and re-layouts, local(): send_rows = jnp.zeros((experts * capacity, model_width), jnp.bfloat16).at...  11.7 us
    concatenate x1, other arithmetic, local(): jnp.concatenate([first, second], axis=1).astype(jnp.bfloat16)  11.5 us
    mul x2, local copies, waits for them, and re-layouts, local(): probs[:, :, None] * out_grad[:, None, :].astype(jnp.float32)  9.48 us
    gather x1, local copies, waits for them, and re-layouts, local(): returned.reshape(-1, model_width)[slots]  7.41 us
    dot_general x1, matrix products, local(): lax.dot_general(expert_rows, both_back, (((0,), (0,)), ((), ())), preferr...  7.15 us
  transfers between devices with their start and end apart: 4, of which 4 were waited for; matrix products, arithmetic and copies ran while one was open for 16% of the time, Pallas kernels for 0%

commit v1 on v0

--- a/solution.py
+++ b/solution.py
@@ -4,7 +4,7 @@
 from jax.sharding import PartitionSpec as P
 
 
-def local(tokens, expert_ids, probs, trade, gate_weight, up_weight, down_weight, out_grad):
+def sparse_local(tokens, expert_ids, probs, trade, gate_weight, up_weight, down_weight, out_grad):
     tok_count, model_width = tokens.shape
     top_count = expert_ids.shape[1]
     hidden_width = gate_weight.shape[2]
@@ -89,6 +89,61 @@
     return (combined, gate_part[None], up_part[None], down_part[None])
 
 
+def dense_local(tokens, expert_ids, probs, trade, gate_weight, up_weight, down_weight, out_grad):
+    hidden_width = gate_weight.shape[2]
+    experts = lax.axis_size("expert")
+    halfway = experts // 2
+    me = lax.axis_index("expert")
+    mine = jnp.where(trade[me % halfway] == 1, jnp.bitwise_xor(me, halfway), me)
+    rows = lax.all_gather(tokens, "expert", axis=0, tiled=True)
+    ids = lax.all_gather(expert_ids, "expert", axis=0, tiled=True)
+    weights = lax.all_gather(probs, "expert", axis=0, tiled=True)
+    grads = lax.all_gather(out_grad, "expert", axis=0, tiled=True)
+    weight = jnp.sum(jnp.where(ids == mine, weights, 0.0), axis=1, keepdims=True)
+    w_gate = gate_weight[0]
+    w_up = up_weight[0]
+    w_down = down_weight[0]
+    gate_act = jnp.dot(rows, w_gate, preferred_element_type=jnp.float32)
+    up_act = jnp.dot(rows, w_up, preferred_element_type=jnp.float32)
+    sigma = jax.nn.sigmoid(gate_act)
+    hidden = (gate_act * sigma * up_act).astype(jnp.bfloat16)
+    expert_out = jnp.dot(hidden, w_down, preferred_element_type=jnp.float32)
+    part = (weight * expert_out).astype(jnp.bfloat16)
+    out_rows = (weight * grads.astype(jnp.float32)).astype(jnp.bfloat16)
+    hidden_grad = lax.dot_general(
+        out_rows, w_down, (((1,), (1,)), ((), ())), preferred_element_type=jnp.float32
+    )
+    gate_back = (hidden_grad * up_act * (sigma * (1.0 + gate_act * (1.0 - sigma)))).astype(
+        jnp.bfloat16
+    )
+    up_back = (hidden_grad * (gate_act * sigma)).astype(jnp.bfloat16)
+    both_back = jnp.concatenate([gate_back, up_back], axis=1)
+    first = lax.dot_general(
+        rows, both_back, (((0,), (0,)), ((), ())), preferred_element_type=jnp.float32
+    )
+    second = lax.dot_general(
+        out_rows, hidden, (((0,), (0,)), ((), ())), preferred_element_type=jnp.float32
+    )
+    summed = lax.psum_scatter(
+        jnp.concatenate([first, second], axis=1).astype(jnp.bfloat16),
+        "dp",
+        scatter_dimension=0,
+        tiled=True,
+    )
+    combined = lax.psum_scatter(part, "expert", scatter_dimension=0, tiled=True)
+    gate_part = summed[:, :hidden_width]
+    up_part = summed[:, hidden_width : 2 * hidden_width]
+    down_part = summed[:, 2 * hidden_width :].T
+    return (combined, gate_part[None], up_part[None], down_part[None])
+
+
+def local(tokens, expert_ids, *rest):
+    capacity = 5 * tokens.shape[0] * expert_ids.shape[1] // (4 * lax.axis_size("expert"))
+    if tokens.shape[0] <= 2 * capacity:
+        return dense_local(tokens, expert_ids, *rest)
+    return sparse_local(tokens, expert_ids, *rest)
+
+
 def solution(mesh):
     return jax.shard_map(
         local,

time: 312 us -> 298 us (0.955); the launches traced: 306 us -> 298 us
  local copies, waits for them, and re-layouts: 55.3 us -> 8.9 us
  waiting for transfers between devices: 161 us -> 193 us
  blocking collectives: 0 us -> 28 us
  starting transfers between devices: 16.2 us -> 0.16 us
  other arithmetic: 27 us -> 11.6 us
  matrix products: 31.9 us -> 41.2 us
    all_to_all x3 -> x0, waiting for transfers between devices: 160 us -> none  [the longest x1 60.3 us: local(): lax.all_to_all(expert_out, 'expert', split_axis=0, concat_axis=0, tiled=T...]
    reduce_scatter x1 -> x2, waiting for transfers between devices: 1.82 us -> 132 us  [the longest x1 87 us: dense_local(): lax.psum_scatter(jnp.concatenate([first, second], axis=1).astype(jnp.bflo...]
    all_gather x0 -> x2, waiting for transfers between devices: none -> 59.6 us  [the longest x1 38.9 us: dense_local(): grads = lax.all_gather(out_grad, 'expert', axis=0, tiled=True)]
    all_gather x0 -> x2, blocking collectives: none -> 28 us  [the longest x1 14.7 us: dense_local(): weights = lax.all_gather(probs, 'expert', axis=0, tiled=True)]
    gather x5 -> x0, local copies, waits for them, and re-layouts: 19.9 us -> none  [the longest x1 7.41 us: local(): returned.reshape(-1, model_width)[slots]]
    all_to_all x3 -> x0, starting transfers between devices: 16 us -> none  [the longest x1 6.93 us: local(): lax.all_to_all(send_grads, 'expert', split_axis=0, concat_axis=0, tiled=T...]
    scatter x1 -> x0, local copies, waits for them, and re-layouts: 11.7 us -> none  [local(): send_rows = jnp.zeros((experts * capacity, model_width), jnp.bfloat16).at...]
    mul x5 -> x0, local copies, waits for them, and re-layouts: 9.81 us -> none  [the longest x2 9.48 us: local(): probs[:, :, None] * out_grad[:, None, :].astype(jnp.float32)]
  transfers between devices with their start and end apart: 4 -> 4, of which waited for: 4 -> 4; matrix products, arithmetic and copies ran while one was open for 16% -> 8% of each run, Pallas kernels for 0% -> 0%
where the time goes in v1:
time: 298 us
  waiting for transfers between devices  193 us (65%)
  matrix products  41.2 us (14%)
  blocking collectives  28 us (9%)
  between operations  14.5 us (5%)
  other arithmetic  11.6 us (4%)
  local copies, waits for them, and re-layouts  8.9 us (3%)
    reduce_scatter x1, waiting for transfers between devices, dense_local(): lax.psum_scatter(jnp.concatenate([first, second], axis=1).astype(jnp.bflo...  87 us
    reduce_scatter x1, waiting for transfers between devices, dense_local(): combined = lax.psum_scatter(part, 'expert', scatter_dimension=0, tiled=True)  45 us
    all_gather x1, waiting for transfers between devices, dense_local(): grads = lax.all_gather(out_grad, 'expert', axis=0, tiled=True)  38.9 us
    all_gather x1, waiting for transfers between devices, dense_local(): rows = lax.all_gather(tokens, 'expert', axis=0, tiled=True)  20.7 us
    all_gather x1, blocking collectives, dense_local(): weights = lax.all_gather(probs, 'expert', axis=0, tiled=True)  14.7 us
    all_gather x1, blocking collectives, dense_local(): ids = lax.all_gather(expert_ids, 'expert', axis=0, tiled=True)  13.3 us
    concatenate x1, other arithmetic, dense_local(): jnp.concatenate([first, second], axis=1).astype(jnp.bfloat16)  11.6 us
    dot_general x1, matrix products, dense_local(): lax.dot_general(rows, both_back, (((0,), (0,)), ((), ())), preferred_elem...  8.5 us
  transfers between devices with their start and end apart: 4, of which 4 were waited for; matrix products, arithmetic and copies ran while one was open for 8% of the time, Pallas kernels for 0%

profile of v1, /device:TPU:0, one launch (start us, length us, event | category | flops | bytes accessed | tf_op | source)
XLA Modules:
  0.0 297.5 jit_solution(16371395438921488804)
XLA Ops:
  7.2 0.0 copy-start
  7.2 0.0 all-gather.3.cloned.1.call-start
  7.2 0.7 all-gather.3.cloned.1.call-update
  7.9 0.0 all-gather.5.cloned.1.call-start
  8.0 0.7 all-gather.5.cloned.1.call-update
  8.7 0.0 reduce-scatter.5.cloned.1.call-start
  8.7 1.2 dynamic_slice.3
  10.6 14.7 %all_gather.13 = f32[1024,4]{0,1:T(4,128)S(1)} all-gather(f32[128,4]{0,1:T(4,128)} %param.10), channel_id=1, replica_groups=mesh['dp'=4,'expert'=8] {'expert'}, dimensions={0}, use_global_device_ids=true | all-gather | bytes 18432 | tf_op jit(solution)/shard_map/all_gather | solution.py:100
  25.3 13.3 %all_gather.12 = s32[1024,4]{0,1:T(4,128)S(1)} all-gather(s32[128,4]{0,1:T(4,128)} %param.9), channel_id=1, replica_groups=mesh['dp'=4,'expert'=8] {'expert'}, dimensions={0}, use_global_device_ids=true | all-gather | bytes 18432 | tf_op jit(solution)/shard_map/all_gather | solution.py:99
  38.7 20.7 %all-gather.3.cloned.1.call-done = bf16[1024,2048]{1,0:T(8,128)(2,1)} async-done(((bf16[128,2048]{1,0:T(8,128)(2,1)}), bf16[1024,2048]{1,0:T(8,128)(2,1)}) %all-gather.3.cloned.1.call-update) | async-done | bytes 4194320 | tf_op jit(solution)/shard_map/all_gather | solution.py:98
  59.4 8.3 %fusion.7 = f32[1024,768]{0,1:T(8,128)} fusion(bf16[1024,2048]{1,0:T(8,128)(2,1)} %all-gather.3.cloned.1.call-done, bf16[1,2048,768]{2,1,0:T(8,128)(2,1)} %param.13), kind=kOutput, calls=%fused_computation.12 | convolution fusion | flops 3221225472 | bytes 10485760 | tf_op jit(solution)/shard_map/dot_general | solution.py:107
  67.7 38.9 %all-gather.5.cloned.1.call-done = bf16[1024,2048]{1,0:T(8,128)(2,1)} async-done(((bf16[128,2048]{1,0:T(8,128)(2,1)}), bf16[1024,2048]{1,0:T(8,128)(2,1)}) %all-gather.5.cloned.1.call-update) | async-done | bytes 4194320 | tf_op jit(solution)/shard_map/all_gather | solution.py:101
  106.6 0.0 copy-done
  106.6 0.0 copy-start.1
  106.7 0.0 copy-start.3
  106.7 5.8 %fusion.4 = f32[1024,768]{0,1:T(8,128)S(1)} fusion(bf16[1,768,2048]{2,1,0:T(8,128)(2,1)S(1)} %copy-done, bf16[1024,2048]{1,0:T(8,128)(2,1)} %all-gather.5.cloned.1.call-done, f32[1024]{0:T(1024)S(1)} %select_reduce_fusion), kind=kOutput, calls=%fused_computation.9 | convolution fusion | flops 3227516928 | bytes 10489856 | tf_op jit(solution)/shard_map/dot_general | solution.py:113
  112.5 0.0 copy-done.1
  112.5 0.0 copy-done.3
  112.5 0.0 copy-start.2
  112.5 7.9 %multiply_convert_fusion.3 = (bf16[1024,768]{0,1:T(8,128)(2,1)}, bf16[1024,768]{0,1:T(8,128)(2,1)}, bf16[1024,768]{0,1:T(8,128)(2,1)S(1)}) fusion(f32[1024,768]{0,1:T(8,128)S(1)} %fusion.4, f32[1024,768]{0,1:T(8,128)} %fusion.7, bf16[1024,2048]{1,0:T(8,128)(2,1)S(1)} %copy-done.1, bf16[1,2048,768]{2,1,0:T(8,128)(2,1)S(1)} %copy-done.3), kind=kOutput, calls=%fused_computation.17 | convolution fusion | flops 3233021952 | bytes 18350080 | tf_op jit(solution)/shard_map/dot_general | solution.py:106
  120.4 0.0 copy-start.4
  120.4 0.0 copy-done.2
  120.4 0.0 copy-start.5
  120.4 0.0 copy-start.6
  120.4 3.9 %convolution_convert_fusion.1 = bf16[2048,768]{0,1:T(8,128)(2,1)S(1)} fusion(bf16[1024,768]{0,1:T(8,128)(2,1)S(1)} %get-tuple-element.10, bf16[1024,2048]{1,0:T(8,128)(2,1)S(1)} %copy-done.2, f32[1024]{0:T(1024)S(1)} %select_reduce_fusion), kind=kOutput, calls=%fused_computation.5 | convolution fusion | flops 3229089792 | bytes 8916992 | tf_op jit(solution)/shard_map/dot_general | solution.py:124
  124.3 0.0 copy-done.4
  124.3 0.0 copy-done.5
  124.3 0.0 copy-done.6
  124.3 8.5 %fusion = bf16[2048,1536]{0,1:T(8,128)(2,1)S(1)} fusion(bf16[1024,2048]{1,0:T(8,128)(2,1)S(1)} %copy-done.1, bf16[1024,768]{0,1:T(8,128)(2,1)S(1)} %copy-done.6, bf16[1024,768]{0,1:T(8,128)(2,1)S(1)} %copy-done.5), kind=kOutput, calls=%fused_computation.4 | convolution fusion | flops 6451888128 | bytes 13631488 | tf_op jit(solution)/shard_map/dot_general | solution.py:121
  132.8 11.6 %pad_maximum_fusion = bf16[2048,2304]{0,1:T(8,128)(2,1)} fusion(bf16[2048,768]{0,1:T(8,128)(2,1)S(1)} %convolution_convert_fusion.1, bf16[2048,1536]{0,1:T(8,128)(2,1)S(1)} %fusion), kind=kLoop, calls=%fused_computation | loop fusion | flops 18874368 | bytes 18874368 | tf_op jit(solution)/shard_map/concatenate | solution.py:128
  144.4 0.0 reduce-scatter.5.cloned.1.call-update
  144.5 0.0 reduce-scatter.3.cloned.1.call-start
  144.5 6.7 %multiply_convert_fusion.1 = bf16[1024,2048]{1,0:T(8,128)(2,1)} fusion(bf16[1024,768]{0,1:T(8,128)(2,1)} %copy-done.4, f32[1024]{0:T(1024)S(1)} %select_reduce_fusion, bf16[1,768,2048]{2,1,0:T(8,128)(2,1)S(1)} %copy-done), kind=kOutput, calls=%fused_computation.2 | convolution fusion | flops 3225419776 | bytes 8916992 | tf_op jit(solution)/shard_map/dot_general | solution.py:110
  151.2 0.0 reduce-scatter.3.cloned.1.call-update
  151.3 87.0 %reduce-scatter.5.cloned.1.call-done = bf16[512,2304]{0,1:T(8,128)(2,1)} async-done(((bf16[2048,2304]{0,1:T(8,128)(2,1)}), bf16[512,2304]{0,1:T(8,128)(2,1)}) %reduce-scatter.5.cloned.1.call-update) | async-done | bytes 2359312 | tf_op jit(solution)/shard_map/reduce_scatter | solution.py:127
  238.3 3.1 %slice_bitcast_fusion = (bf16[1,768,512]{2,1,0:T(8,128)(2,1)}, bf16[1,512,768]{1,2,0:T(8,128)(2,1)}, bf16[1,512,768]{1,2,0:T(8,128)(2,1)}) fusion(bf16[512,2304]{0,1:T(8,128)(2,1)} %reduce-scatter.5.cloned.1.call-done), kind=kLoop, calls=%fused_computation.21 | loop fusion | bytes 4718592 | tf_op jit(solution)/shard_map/broadcast_in_dim | solution.py:137
  241.4 2.3 copy.12
  243.7 2.3 copy.13
  245.9 45.0 %reduce-scatter.3.cloned.1.call-done = bf16[128,2048]{1,0:T(8,128)(2,1)} async-done(((bf16[1024,2048]{1,0:T(8,128)(2,1)}), bf16[128,2048]{1,0:T(8,128)(2,1)}) %reduce-scatter.3.cloned.1.call-update) | async-done | bytes 524304 | tf_op jit(solution)/shard_map/reduce_scatter | solution.py:133
  (1 shorter events, 0.0 us)
Async XLA Ops:
  7.2 99.5 %copy-start = (bf16[1,768,2048]{2,1,0:T(8,128)(2,1)S(1)}, bf16[1,768,2048]{2,1,0:T(8,128)(2,1)}, u32[]{:S(2)}) copy-start(bf16[1,768,2048]{2,1,0:T(8,128)(2,1)} %param.14) | copy-start | bytes 9437188
  7.2 52.2 %all-gather.3.cloned.1.call-start = ((), (), s32[]{:S(2)}) async-start(), calls=%async_computation.2 | async-start | bytes 4718592 | tf_op jit(solution)/shard_map/all_gather | solution.py:98
  7.9 98.7 %all-gather.5.cloned.1.call-start = ((), (), s32[]{:S(2)}) async-start(), calls=%async_computation.4 | async-start | bytes 4718592 | tf_op jit(solution)/shard_map/all_gather | solution.py:101
  8.7 229.7 %reduce-scatter.5.cloned.1.call-start = ((), (), s32[]{:S(2)}) async-start(), calls=%async_computation.5 | async-start | bytes 11796480 | tf_op jit(solution)/shard_map/reduce_scatter | solution.py:127
  106.6 5.8 %copy-start.1 = (bf16[1024,2048]{1,0:T(8,128)(2,1)S(1)}, bf16[1024,2048]{1,0:T(8,128)(2,1)}, u32[]{:S(2)}) copy-start(bf16[1024,2048]{1,0:T(8,128)(2,1)} %all-gather.3.cloned.1.call-done) | copy-start | bytes 12582916
  106.7 5.9 %copy-start.3 = (bf16[1,2048,768]{2,1,0:T(8,128)(2,1)S(1)}, bf16[1,2048,768]{2,1,0:T(8,128)(2,1)}, u32[]{:S(2)}) copy-start(bf16[1,2048,768]{2,1,0:T(8,128)(2,1)} %param.12) | copy-start | bytes 9437188
  112.5 7.9 %copy-start.2 = (bf16[1024,2048]{1,0:T(8,128)(2,1)S(1)}, bf16[1024,2048]{1,0:T(8,128)(2,1)}, u32[]{:S(2)}) copy-start(bf16[1024,2048]{1,0:T(8,128)(2,1)} %all-gather.5.cloned.1.call-done) | copy-start | bytes 12582916
  120.4 3.9 %copy-start.4 = (bf16[1024,768]{0,1:T(8,128)(2,1)}, bf16[1024,768]{0,1:T(8,128)(2,1)S(1)}, u32[]{:S(2)}) copy-start(bf16[1024,768]{0,1:T(8,128)(2,1)S(1)} %get-tuple-element.10) | copy-start | bytes 4718596
  120.4 3.9 %copy-start.5 = (bf16[1024,768]{0,1:T(8,128)(2,1)S(1)}, bf16[1024,768]{0,1:T(8,128)(2,1)}, u32[]{:S(2)}) copy-start(bf16[1024,768]{0,1:T(8,128)(2,1)} %get-tuple-element.8) | copy-start | bytes 4718596
  120.4 3.9 %copy-start.6 = (bf16[1024,768]{0,1:T(8,128)(2,1)S(1)}, bf16[1024,768]{0,1:T(8,128)(2,1)}, u32[]{:S(2)}) copy-start(bf16[1024,768]{0,1:T(8,128)(2,1)} %get-tuple-element.9) | copy-start | bytes 4718596
  144.5 146.5 %reduce-scatter.3.cloned.1.call-start = ((), (), s32[]{:S(2)}) async-start(), calls=%async_computation.3 | async-start | bytes 4718592 | tf_op jit(solution)/shard_map/reduce_scatter | solution.py:133
Sparse Core Ops, SparseCore 0:
  9.6 49.7 all-gather.2
  61.0 45.6 all-gather.4
  144.6 93.6 reduce-scatter.4
  241.0 49.8 reduce-scatter.2

commit v2 on v0

--- a/solution.py
+++ b/solution.py
@@ -1,10 +1,13 @@
+import functools
 import jax
 import jax.numpy as jnp
 from jax import lax
+from jax.experimental import pallas as pl
+from jax.experimental.pallas import tpu as pltpu
 from jax.sharding import PartitionSpec as P
 
 
-def local(tokens, expert_ids, probs, trade, gate_weight, up_weight, down_weight, out_grad):
+def sparse_local(tokens, expert_ids, probs, trade, gate_weight, up_weight, down_weight, out_grad):
     tok_count, model_width = tokens.shape
     top_count = expert_ids.shape[1]
     hidden_width = gate_weight.shape[2]
@@ -87,6 +90,464 @@
     up_part = summed[:, hidden_width : 2 * hidden_width]
     down_part = summed[:, 2 * hidden_width :].T
     return (combined, gate_part[None], up_part[None], down_part[None])
+
+
+def layer_kernel(
+    tokens, grads, weights, wg_hbm, wu_hbm, wd_hbm, combined, gate_out, up_out, down_out,
+    rows, cots, wts, wg, wu, wd, wcol, hidden, back, acc, pairs, part, sib_part, far_part,
+    gu, dn, gu_x, gu_y, dn_x, dn_y, gu_two, dn_two,
+    load_sem, tok_send, tok_sib, tok_recv, cot_send, cot_sib, cot_recv, wt_send, wt_recv,
+    part_sib, part_sib_recv, part_send, part_recv, red_send, red_recv,
+):
+    f32 = jnp.float32
+    bf16 = jnp.bfloat16
+    experts = lax.axis_size("expert")
+    chips = experts // 2
+    last = chips - 1
+    replicas = lax.axis_size("dp")
+    count, width = tokens.shape
+    share = width // replicas
+    ff = wg.shape[1]
+    me = lax.axis_index("expert")
+    z = me // 2
+    c = me % 2
+    d = lax.axis_index("dp")
+    dx = (d // 2) * 2 + (1 - d % 2)
+    dy = (1 - d // 2) * 2 + d % 2
+    dd = 3 - d
+    upper = z // (chips // 2)
+    zm = z * (1 - upper) + (last - z) * upper
+    sibling = z * 2 + (1 - c)
+    inner = zm == 1
+
+    def at_chip(m):
+        return m * (1 - upper) + (last - m) * upper
+
+    def other(q):
+        return at_chip(jnp.where(q == 0, zm, jnp.where(q == 1, 1 - zm, q)))
+
+    def owner_of(p):
+        return jnp.where(p == 0, dd, jnp.where(p == 1, dx, jnp.where(p == 2, dy, d)))
+
+    def lanes(p):
+        return pl.ds(pl.multiple_of(owner_of(p) * share, share), share)
+
+    def remote(src, dst, ssem, rsem, axis, to):
+        return pltpu.make_async_remote_copy(
+            src_ref=src, dst_ref=dst, send_sem=ssem, recv_sem=rsem,
+            device_id={axis: to}, device_id_type=pl.DeviceIdType.MESH,
+        )
+
+    loads = [
+        pltpu.make_async_copy(wg_hbm, wg, load_sem.at[0]),
+        pltpu.make_async_copy(wu_hbm, wu, load_sem.at[1]),
+        pltpu.make_async_copy(wd_hbm, wd, load_sem.at[2]),
+        pltpu.make_async_copy(tokens, rows.at[me], load_sem.at[3]),
+        pltpu.make_async_copy(weights, wts.at[me], load_sem.at[4]),
+    ]
+    loads[3].start()
+    loads[4].start()
+
+    def cot_load(p):
+        return pltpu.make_async_copy(grads.at[:, lanes(p)], cots.at[p, me], load_sem.at[5 + p])
+
+    for load in loads[:3]:
+        load.start()
+    for p in range(replicas):
+        cot_load(p).start()
+
+    barrier = pltpu.get_barrier_semaphore()
+    for r in range(1, experts):
+        pl.semaphore_signal(
+            barrier, inc=1, device_id={"expert": (me + r) % experts},
+            device_id_type=pl.DeviceIdType.MESH,
+        )
+    for to in (dx, dy):
+        pl.semaphore_signal(
+            barrier, inc=1, device_id={"dp": to}, device_id_type=pl.DeviceIdType.MESH
+        )
+    pl.semaphore_wait(barrier, experts + 1)
+
+    def tok_copy(q):
+        to = other(q) * 2 + c
+        return remote(tokens, rows.at[me], tok_send.at[q], tok_recv.at[me], "expert", to)
+
+    def cot_copy(p, q):
+        to = other(q) * 2 + c
+        return remote(
+            grads.at[:, lanes(p)], cots.at[p, me], cot_send.at[p, q], cot_recv.at[p, me],
+            "expert", to,
+        )
+
+    def each_target(fn):
+        for q in range(1, chips):
+            if q < last:
+                fn(q)
+            else:
+                pl.when(inner)(functools.partial(fn, q))
+
+    each_target(lambda q: tok_copy(q).start())
+
+    def wt_copy(r):
+        return remote(
+            weights, wts.at[me], wt_send.at[r], wt_recv.at[me], "expert", (me + r) % experts
+        )
+
+    for r in range(1, experts):
+        wt_copy(r).start()
+
+    end = at_chip(0) * 2 + c
+
+    def tok_from(slot):
+        return remote(rows.at[slot], rows.at[slot], tok_send.at[0], tok_recv.at[slot], "expert", end)
+
+    def tok_to_sib(zp):
+        slot = zp * 2 + c
+        return remote(
+            rows.at[slot], rows.at[slot], tok_sib.at[zp], tok_recv.at[slot], "expert", sibling
+        )
+
+    def cot_from(p, slot):
+        ref = cots.at[p, slot]
+        return remote(ref, ref, cot_send.at[p, 0], cot_recv.at[p, slot], "expert", end)
+
+    def cot_to_sib(p, zp):
+        slot = zp * 2 + c
+        ref = cots.at[p, slot]
+        return remote(ref, ref, cot_sib.at[p, zp], cot_recv.at[p, slot], "expert", sibling)
+
+    def part_to_sib(zp):
+        return remote(
+            part.at[zp * 2 + (1 - c)], sib_part.at[zp], part_sib.at[zp], part_sib_recv.at[zp],
+            "expert", sibling,
+        )
+
+    loads[4].wait()
+    for r in range(1, experts):
+        slot = (me + r) % experts
+        remote(weights, wts.at[slot], wt_send.at[r], wt_recv.at[slot], "expert", slot).wait_recv()
+    eye = lax.broadcasted_iota(jnp.int32, (count, count), 0) == lax.broadcasted_iota(
+        jnp.int32, (count, count), 1
+    )
+    for slot in range(experts):
+        row = jnp.broadcast_to(wts[slot, pl.ds(me, 1), :], (count, count))
+        column = jnp.sum(jnp.where(eye, row, 0.0), axis=1, keepdims=True)
+        wcol[pl.ds(slot * count, count), :] = jnp.broadcast_to(column, (count, wcol.shape[1]))
+
+    pair = 2 * count
+
+    @pl.loop(0, chips)
+    def _(q):
+        zp = other(q)
+
+        @pl.when(q == 0)
+        def _():
+            loads[3].wait()
+
+        @pl.when(q > 0)
+        def _():
+            tok_from(zp * 2 + c).wait_recv()
+
+        tok_to_sib(zp).start()
+
+        @pl.when(jnp.logical_and(inner, q == last))
+        def _():
+            tok_from(zp * 2 + c).start()
+
+        @pl.when(q == 0)
+        def _():
+            for load in loads[:3]:
+                load.wait()
+
+        @pl.when(q == last)
+        def _():
+            for p in range(2):
+                each_target(lambda q: cot_copy(p, q).start())
+
+        tok_from(zp * 2 + (1 - c)).wait_recv()
+        where = pl.ds(pl.multiple_of(zp * pair, pair), pair)
+        x = rows[pl.ds(zp * 2, 2)].reshape(pair, width)
+        tile = ff // 3
+
+        @pl.loop(0, 3)
+        def _(n):
+            cols = pl.ds(pl.multiple_of(n * tile, tile), tile)
+            g = jnp.dot(x, wg[:, cols], preferred_element_type=f32)
+            u = jnp.dot(x, wu[:, cols], preferred_element_type=f32)
+            sigma = jax.nn.sigmoid(g)
+            silu = g * sigma
+            hidden[where, cols] = (silu * u).astype(bf16)
+            back[where, cols] = (u * (sigma * (1.0 + g * (1.0 - sigma)))).astype(bf16)
+            back[where, pl.ds(pl.multiple_of(ff + n * tile, tile), tile)] = silu.astype(bf16)
+
+        @pl.loop(0, replicas)
+        def _(n):
+            cols = pl.ds(pl.multiple_of(n * share, share), share)
+            o = jnp.dot(hidden[where, :], wd[:, cols], preferred_element_type=f32)
+            o = (o * wcol[where, 0:1]).astype(bf16)
+            part[zp * 2, :, cols] = o[:count]
+            part[zp * 2 + 1, :, cols] = o[count:]
+
+        part_to_sib(zp).start()
+
+    half = share // 2
+    fhalf = ff // 2
+
+    def reduce_copy(step, wide):
+        send, far = (gu, (gu_x, gu_y, gu_two)) if wide else (dn, (dn_x, dn_y, dn_two))
+        h = half if wide else fhalf
+        lo, hi = pl.ds(0, h), pl.ds(h, h)
+        src, dst, axis_to = {
+            0: (send.at[0, lo], far[0].at[0], dx),
+            1: (send.at[0, hi], far[1].at[0], dy),
+            2: (send.at[1, lo], far[0].at[1], dx),
+            3: (send.at[2, hi], far[1].at[1], dy),
+            4: (send.at[2, lo], far[2].at[0], dy),
+            5: (send.at[1, hi], far[2].at[1], dx),
+        }[step]
+        k = step + 6 * int(wide)
+        return remote(src, dst, red_send.at[k], red_recv.at[k], "dp", axis_to)
+
+    def reduce_step(p, wide):
+        send, far = (gu, (gu_x, gu_y)) if wide else (dn, (dn_x, dn_y))
+        h = half if wide else fhalf
+        lo, hi = pl.ds(0, h), pl.ds(h, h)
+
+        @pl.when(p == 0)
+        def _():
+            reduce_copy(0, wide).start()
+            reduce_copy(1, wide).start()
+
+        @pl.when(p == 1)
+        def _():
+            reduce_copy(2, wide).start()
+
+        @pl.when(p == 2)
+        def _():
+            reduce_copy(3, wide).start()
+
+        @pl.when(p == 3)
+        def _():
+            reduce_copy(0, wide).wait_recv()
+            send[2, lo] = (send[2, lo].astype(f32) + far[0][0].astype(f32)).astype(bf16)
+            reduce_copy(4, wide).start()
+            reduce_copy(1, wide).wait_recv()
+            send[1, hi] = (send[1, hi].astype(f32) + far[1][0].astype(f32)).astype(bf16)
+            reduce_copy(5, wide).start()
+
+    @pl.loop(0, replicas)
+    def _(p):
+        for q in range(chips):
+            zp = other(q)
+            if q == 0:
+                cot_load(p).wait()
+            else:
+                cot_from(p, zp * 2 + c).wait_recv()
+            cot_to_sib(p, zp).start()
+            if q == last:
+
+                @pl.when(inner)
+                def _():
+                    cot_from(p, zp * 2 + c).start()
+
+        @pl.when(p < replicas - 2)
+        def _():
+            each_target(lambda q: cot_copy(p + 2, q).start())
+
+        for zp in range(chips):
+            cot_from(p, zp * 2 + (1 - c)).wait_recv()
+        for slot in range(experts):
+            where = pl.ds(slot * count, count)
+            pairs[where, :] = (wcol[where, 0:1] * cots[p, slot].astype(f32)).astype(bf16)
+        tile = ff // 3
+
+        @pl.loop(0, 3)
+        def _(n):
+            cols = pl.ds(pl.multiple_of(n * tile, tile), tile)
+            dn[p, cols, :] = lax.dot_general(
+                hidden[:, cols], pairs[...], (((0,), (0,)), ((), ())), preferred_element_type=f32
+            ).astype(bf16)
+
+        reduce_step(p, False)
+
+        @pl.loop(0, 3)
+        def _(n):
+            cols = pl.ds(pl.multiple_of(n * tile, tile), tile)
+            more = lax.dot_general(
+                pairs[...], wd[cols, lanes(p)], (((1,), (1,)), ((), ())),
+                preferred_element_type=f32,
+            )
+            acc[:, cols] = jnp.where(p == 0, more, acc[:, cols] + more)
+
+    @pl.loop(0, experts)
+    def _(n):
+        where = pl.ds(pl.multiple_of(n * count, count), count)
+        back[where, :ff] = (acc[where, :] * back[where, :ff].astype(f32)).astype(bf16)
+        back[where, ff:] = (acc[where, :] * back[where, ff:].astype(f32)).astype(bf16)
+
+    def part_copy(q):
+        zp = other(q)
+        return remote(
+            part.at[zp * 2 + c], far_part.at[z], part_send.at[q], part_recv.at[z], "expert",
+            zp * 2 + c,
+        )
+
+    for q in (0,) + tuple(range(last, 0, -1)):
+        zp = other(q)
+        remote(
+            part.at[zp * 2 + (1 - c)], sib_part.at[zp], part_sib.at[zp], part_sib_recv.at[zp],
+            "expert", sibling,
+        ).wait_recv()
+        part[zp * 2 + c] = (
+            part[zp * 2 + c].astype(f32) + sib_part[zp].astype(f32)
+        ).astype(bf16)
+        if q > 0:
+            part_copy(q).start()
+
+    @pl.loop(0, replicas)
+    def _(p):
+        for h in range(2):
+            cols = pl.ds(pl.multiple_of(owner_of(p) * share + h * half, half), half)
+            lhs = rows[:, :, cols].reshape(experts * count, half)
+            for n in range(2):
+                gu[p, h * half:(h + 1) * half, n * ff:(n + 1) * ff] = lax.dot_general(
+                    lhs, back[:, n * ff:(n + 1) * ff], (((0,), (0,)), ((), ())),
+                    preferred_element_type=f32,
+                ).astype(bf16)
+        reduce_step(p, True)
+
+    def finish(wide):
+        for k in (2, 3, 4, 5):
+            reduce_copy(k, wide).wait_recv()
+
+    def total(own, one, two):
+        return (own.astype(f32) + one.astype(f32) + two.astype(f32)).astype(bf16)
+
+    finish(False)
+    down_out[:fhalf] = total(dn[3, :fhalf], dn_x[1], dn_two[0])
+    down_out[fhalf:] = total(dn[3, fhalf:], dn_y[1], dn_two[1])
+    for q in range(1, chips):
+        zp = other(q)
+        remote(
+            part.at[zp * 2 + c], far_part.at[zp], part_send.at[q], part_recv.at[zp], "expert",
+            zp * 2 + c,
+        ).wait_recv()
+    mixed = part[me].astype(f32)
+    for q in range(1, chips):
+        mixed = mixed + far_part[other(q)].astype(f32)
+    combined[...] = mixed.astype(bf16)
+    finish(True)
+    for n, out in ((0, gate_out), (1, up_out)):
+        cols = slice(n * ff, (n + 1) * ff)
+        out[:half] = total(gu[3, :half, cols], gu_x[1, :, cols], gu_two[0, :, cols])
+        out[half:] = total(gu[3, half:, cols], gu_y[1, :, cols], gu_two[1, :, cols])
+
+    each_target(lambda q: tok_copy(q).wait_send())
+    for p in range(replicas):
+        each_target(lambda q: cot_copy(p, q).wait_send())
+    for r in range(1, experts):
+        wt_copy(r).wait_send()
+    for q in range(chips):
+        zp = other(q)
+        tok_to_sib(zp).wait_send()
+        part_to_sib(zp).wait_send()
+        for p in range(replicas):
+            cot_to_sib(p, zp).wait_send()
+        if q > 0:
+            part_copy(q).wait_send()
+
+    @pl.when(inner)
+    def _():
+        slot = other(last) * 2 + c
+        tok_from(slot).wait_send()
+        for p in range(replicas):
+            cot_from(p, slot).wait_send()
+
+    for wide in (False, True):
+        for k in range(6):
+            reduce_copy(k, wide).wait_send()
+
+
+def chain_local(tokens, expert_ids, probs, trade, gate_weight, up_weight, down_weight, out_grad):
+    count, width = tokens.shape
+    ff = gate_weight.shape[2]
+    experts = lax.axis_size("expert")
+    replicas = lax.axis_size("dp")
+    chips = experts // 2
+    share = width // replicas
+    halfway = experts // 2
+    numbers = jnp.arange(experts, dtype=jnp.int32)
+    owners = jnp.where(trade[numbers % halfway] == 1, jnp.bitwise_xor(numbers, halfway), numbers)
+    weights = jnp.sum(
+        jnp.where(expert_ids.T[None] == owners[:, None, None], probs.T[None], 0.0), axis=1
+    )
+    bf16, f32 = jnp.bfloat16, jnp.float32
+    dma = pltpu.SemaphoreType.DMA
+    total = experts * count
+    hbm = pl.BlockSpec(memory_space=pl.ANY)
+    vmem = pl.BlockSpec(memory_space=pltpu.VMEM)
+    combined, gate, up, down = pl.pallas_call(
+        layer_kernel,
+        out_shape=(
+            jax.ShapeDtypeStruct((count, width), bf16),
+            jax.ShapeDtypeStruct((share, ff), bf16),
+            jax.ShapeDtypeStruct((share, ff), bf16),
+            jax.ShapeDtypeStruct((ff, share), bf16),
+        ),
+        in_specs=[hbm] * 6,
+        out_specs=(vmem,) * 4,
+        scratch_shapes=[
+            pltpu.VMEM((experts, count, width), bf16),
+            pltpu.VMEM((replicas, experts, count, share), bf16),
+            pltpu.VMEM((experts, experts, count), f32),
+            pltpu.VMEM((width, ff), bf16),
+            pltpu.VMEM((width, ff), bf16),
+            pltpu.VMEM((ff, width), bf16),
+            pltpu.VMEM((total, count), f32),
+            pltpu.VMEM((total, ff), bf16),
+            pltpu.VMEM((total, 2 * ff), bf16),
+            pltpu.VMEM((total, ff), f32),
+            pltpu.VMEM((total, share), bf16),
+            pltpu.VMEM((experts, count, width), bf16),
+            pltpu.VMEM((chips, count, width), bf16),
+            pltpu.VMEM((chips, count, width), bf16),
+            pltpu.VMEM((replicas, share, 2 * ff), bf16),
+            pltpu.VMEM((replicas, ff, share), bf16),
+            pltpu.VMEM((2, share // 2, 2 * ff), bf16),
+            pltpu.VMEM((2, share // 2, 2 * ff), bf16),
+            pltpu.VMEM((2, ff // 2, share), bf16),
+            pltpu.VMEM((2, ff // 2, share), bf16),
+            pltpu.VMEM((2, share // 2, 2 * ff), bf16),
+            pltpu.VMEM((2, ff // 2, share), bf16),
+            dma((5 + replicas,)),
+            dma((chips,)),
+            dma((chips,)),
+            dma((experts,)),
+            dma((replicas, chips)),
+            dma((replicas, chips)),
+            dma((replicas, experts)),
+            dma((experts,)),
+            dma((experts,)),
+            dma((chips,)),
+            dma((chips,)),
+            dma((chips,)),
+            dma((chips,)),
+            dma((12,)),
+            dma((12,)),
+        ],
+        compiler_params=pltpu.CompilerParams(
+            collective_id=0, has_side_effects=True, vmem_limit_bytes=67043328
+        ),
+    )(tokens, out_grad, weights, gate_weight[0], up_weight[0], down_weight[0])
+    return combined, gate[None], up[None], down[None]
+
+
+def local(tokens, expert_ids, *rest):
+    experts, replicas = lax.axis_size("expert"), lax.axis_size("dp")
+    capacity = 5 * tokens.shape[0] * expert_ids.shape[1] // (4 * experts)
+    if tokens.shape[0] <= 2 * capacity and experts == 8 and replicas == 4:
+        return chain_local(tokens, expert_ids, *rest)
+    return sparse_local(tokens, expert_ids, *rest)
 
 
 def solution(mesh):

time: 312 us -> 192 us (0.62); the launches traced: 306 us -> 192 us
  Pallas kernels: 0 us -> 183 us
  waiting for transfers between devices: 161 us -> 0 us
  local copies, waits for them, and re-layouts: 55.3 us -> 7.13 us
  matrix products: 31.9 us -> 0 us
  other arithmetic: 27 us -> 1.39 us
  starting transfers between devices: 16.2 us -> 0 us
  between operations: 14.5 us -> 0.67 us
    pallas_call x0 -> x1, Pallas kernels: none -> 183 us  [chain_local(): pl.pallas_call(layer_kernel, out_shape=(jax.ShapeDtypeStruct((count, widt...]
    all_to_all x3 -> x0, waiting for transfers between devices: 160 us -> none  [the longest x1 60.3 us: local(): lax.all_to_all(expert_out, 'expert', split_axis=0, concat_axis=0, tiled=T...]
    dot_general x6 -> x0, matrix products: 31.9 us -> none  [the longest x1 7.15 us: local(): lax.dot_general(expert_rows, both_back, (((0,), (0,)), ((), ())), preferr...]
    gather x5 -> x1, local copies, waits for them, and re-layouts: 19.9 us -> 1.3 us  [chain_local(): trade[numbers % halfway] == 1]
    all_to_all x3 -> x0, starting transfers between devices: 16 us -> none  [the longest x1 6.93 us: local(): lax.all_to_all(send_grads, 'expert', split_axis=0, concat_axis=0, tiled=T...]
    scatter x1 -> x0, local copies, waits for them, and re-layouts: 11.7 us -> none  [local(): send_rows = jnp.zeros((experts * capacity, model_width), jnp.bfloat16).at...]
    concatenate x1 -> x0, other arithmetic: 11.5 us -> none  [local(): jnp.concatenate([first, second], axis=1).astype(jnp.bfloat16)]
    mul x5 -> x0, local copies, waits for them, and re-layouts: 9.81 us -> none  [the longest x2 9.48 us: local(): probs[:, :, None] * out_grad[:, None, :].astype(jnp.float32)]
  transfers between devices with their start and end apart: 4 -> 0, of which waited for: 4 -> 0; matrix products, arithmetic and copies ran while one was open for 16% -> 0% of each run, Pallas kernels for 0% -> 0%
where the time goes in v2:
time: 192 us
  Pallas kernels  183 us (95%)
  local copies, waits for them, and re-layouts  7.13 us (4%)
    pallas_call x1, Pallas kernels, chain_local(): pl.pallas_call(layer_kernel, out_shape=(jax.ShapeDtypeStruct((count, widt...  183 us
    unnamed x8, local copies, waits for them, and re-layouts  5.83 us

profile of v2, /device:TPU:0, one launch (start us, length us, event | category | flops | bytes accessed | tf_op | source)
XLA Modules:
  0.0 192.0 jit_solution(4140688265133110904)
XLA Ops:
  0.7 1.3 gather_fusion
  2.0 1.4 select_reduce_fusion.weights
  3.3 182.8 %shard_map.111 = (bf16[128,2048]{1,0:T(8,128)(2,1)}, bf16[512,768]{1,0:T(8,128)(2,1)}, bf16[512,768]{1,0:T(8,128)(2,1)}, bf16[768,512]{1,0:T(8,128)(2,1)}) custom-call(bf16[128,2048]{1,0:T(8,128)(2,1)} %tokens.1, bf16[128,2048]{1,0:T(8,128)(2,1)} %grads.1, f32[8,128]{1,0:T(8,128)} %select_reduce_fusion.weights, bf16[2048,768]{1,0:T(8,128)(2,1)} %bitcast.10, ...), custom_call_target="tpu_custom_call" | custom-call | tf_op jit(solution)/shard_map/pallas_call | solution.py:489
  186.2 0.0 copy-start.1
  186.2 0.0 copy-start
  186.2 2.0 %copy.16 = bf16[128,2048]{1,0:T(8,128)(2,1)} copy(bf16[128,2048]{1,0:T(8,128)(2,1)} %get-tuple-element.16) | data formatting | bytes 1048576
  188.2 2.1 %copy.17 = bf16[1,512,768]{2,1,0:T(8,128)(2,1)} copy(bf16[1,512,768]{2,1,0:T(8,128)(2,1)} %bitcast.15) | data formatting | bytes 1572864
  190.2 0.0 copy-done.1
  190.2 0.9 copy.18
  191.1 0.0 copy-done
  191.1 0.9 copy.19
  (3 shorter events, 0.0 us)
Async XLA Ops:
  186.2 4.1 %copy-start.1 = (bf16[512,768]{1,0:T(8,128)(2,1)S(1)}, bf16[512,768]{1,0:T(8,128)(2,1)}, u32[]{:S(2)}) copy-start(bf16[512,768]{1,0:T(8,128)(2,1)} %get-tuple-element.10) | copy-start | bytes 2359300
  186.2 5.0 %copy-start = (bf16[768,512]{1,0:T(8,128)(2,1)S(1)}, bf16[768,512]{1,0:T(8,128)(2,1)}, u32[]{:S(2)}) copy-start(bf16[768,512]{1,0:T(8,128)(2,1)} %get-tuple-element.11) | copy-start | bytes 2359300

commit v3 on v2

--- a/solution.py
+++ b/solution.py
@@ -126,6 +126,10 @@
     def other(q):
         return at_chip(jnp.where(q == 0, zm, jnp.where(q == 1, 1 - zm, q)))
 
+    def source(q):
+        m = jnp.where(jnp.logical_and(inner, q >= 2), last + 2 - q, q)
+        return at_chip(jnp.where(q == 0, zm, jnp.where(q == 1, 1 - zm, m)))
+
     def owner_of(p):
         return jnp.where(p == 0, dd, jnp.where(p == 1, dx, jnp.where(p == 2, dy, d)))
 
@@ -186,8 +190,6 @@
             else:
                 pl.when(inner)(functools.partial(fn, q))
 
-    each_target(lambda q: tok_copy(q).start())
-
     def wt_copy(r):
         return remote(
             weights, wts.at[me], wt_send.at[r], wt_recv.at[me], "expert", (me + r) % experts
@@ -195,6 +197,7 @@
 
     for r in range(1, experts):
         wt_copy(r).start()
+    each_target(lambda q: tok_copy(q).start())
 
     end = at_chip(0) * 2 + c
 
@@ -238,7 +241,12 @@
 
     @pl.loop(0, chips)
     def _(q):
-        zp = other(q)
+        zp = source(q)
+
+        @pl.when(q == last)
+        def _():
+            for p in range(2):
+                each_target(lambda q: cot_copy(p, q).start())
 
         @pl.when(q == 0)
         def _():
@@ -248,21 +256,16 @@
         def _():
             tok_from(zp * 2 + c).wait_recv()
 
+        @pl.when(jnp.logical_and(inner, q == last - 1))
+        def _():
+            tok_from(zp * 2 + c).start()
+
         tok_to_sib(zp).start()
-
-        @pl.when(jnp.logical_and(inner, q == last))
-        def _():
-            tok_from(zp * 2 + c).start()
 
         @pl.when(q == 0)
         def _():
             for load in loads[:3]:
                 load.wait()
-
-        @pl.when(q == last)
-        def _():
-            for p in range(2):
-                each_target(lambda q: cot_copy(p, q).start())
 
         tok_from(zp * 2 + (1 - c)).wait_recv()
         where = pl.ds(pl.multiple_of(zp * pair, pair), pair)
@@ -289,6 +292,13 @@
             part[zp * 2 + 1, :, cols] = o[count:]
 
         part_to_sib(zp).start()
+
+    def part_copy(q):
+        zp = other(q)
+        return remote(
+            part.at[zp * 2 + c], far_part.at[z], part_send.at[q], part_recv.at[z], "expert",
+            zp * 2 + c,
+        )
 
     half = share // 2
     fhalf = ff // 2
@@ -326,7 +336,7 @@
         def _():
             reduce_copy(3, wide).start()
 
-        @pl.when(p == 3)
+        @pl.when(p == (3 if wide else 2))
         def _():
             reduce_copy(0, wide).wait_recv()
             send[2, lo] = (send[2, lo].astype(f32) + far[0][0].astype(f32)).astype(bf16)
@@ -338,21 +348,27 @@
     @pl.loop(0, replicas)
     def _(p):
         for q in range(chips):
-            zp = other(q)
+            zp = source(q)
             if q == 0:
                 cot_load(p).wait()
             else:
                 cot_from(p, zp * 2 + c).wait_recv()
-            cot_to_sib(p, zp).start()
-            if q == last:
+            if q == last - 1:
 
                 @pl.when(inner)
                 def _():
                     cot_from(p, zp * 2 + c).start()
 
+            cot_to_sib(p, zp).start()
+
         @pl.when(p < replicas - 2)
         def _():
             each_target(lambda q: cot_copy(p + 2, q).start())
+
+        @pl.when(p == replicas - 1)
+        def _():
+            for q in range(last, 0, -1):
+                part_copy(q).start()
 
         for zp in range(chips):
             cot_from(p, zp * 2 + (1 - c)).wait_recv()
@@ -369,6 +385,17 @@
             ).astype(bf16)
 
         reduce_step(p, False)
+
+        @pl.when(p == 0)
+        def _():
+            for zp in range(chips):
+                remote(
+                    part.at[zp * 2 + (1 - c)], sib_part.at[zp], part_sib.at[zp],
+                    part_sib_recv.at[zp], "expert", sibling,
+                ).wait_recv()
+                part[zp * 2 + c] = (
+                    part[zp * 2 + c].astype(f32) + sib_part[zp].astype(f32)
+                ).astype(bf16)
 
         @pl.loop(0, 3)
         def _(n):
@@ -384,25 +411,6 @@
         where = pl.ds(pl.multiple_of(n * count, count), count)
         back[where, :ff] = (acc[where, :] * back[where, :ff].astype(f32)).astype(bf16)
         back[where, ff:] = (acc[where, :] * back[where, ff:].astype(f32)).astype(bf16)
-
-    def part_copy(q):
-        zp = other(q)
-        return remote(
-            part.at[zp * 2 + c], far_part.at[z], part_send.at[q], part_recv.at[z], "expert",
-            zp * 2 + c,
-        )
-
-    for q in (0,) + tuple(range(last, 0, -1)):
-        zp = other(q)
-        remote(
-            part.at[zp * 2 + (1 - c)], sib_part.at[zp], part_sib.at[zp], part_sib_recv.at[zp],
-            "expert", sibling,
-        ).wait_recv()
-        part[zp * 2 + c] = (
-            part[zp * 2 + c].astype(f32) + sib_part[zp].astype(f32)
-        ).astype(bf16)
-        if q > 0:
-            part_copy(q).start()
 
     @pl.loop(0, replicas)
     def _(p):
@@ -458,7 +466,7 @@
 
     @pl.when(inner)
     def _():
-        slot = other(last) * 2 + c
+        slot = source(last - 1) * 2 + c
         tok_from(slot).wait_send()
         for p in range(replicas):
             cot_from(p, slot).wait_send()
@@ -477,7 +485,9 @@
     share = width // replicas
     halfway = experts // 2
     numbers = jnp.arange(experts, dtype=jnp.int32)
-    owners = jnp.where(trade[numbers % halfway] == 1, jnp.bitwise_xor(numbers, halfway), numbers)
+    owners = jnp.where(
+        jnp.concatenate([trade, trade]) == 1, jnp.bitwise_xor(numbers, halfway), numbers
+    )
     weights = jnp.sum(
         jnp.where(expert_ids.T[None] == owners[:, None, None], probs.T[None], 0.0), axis=1
     )

time: 192 us -> 174 us (0.906)
  Pallas kernels: 183 us -> 165 us
    pallas_call x1, Pallas kernels: 183 us -> 165 us  [chain_local(): pl.pallas_call(layer_kernel, out_shape=(jax.ShapeDtypeStruct((count, widt...]
where the time goes in v3:
time: 174 us
  Pallas kernels  165 us (95%)
  local copies, waits for them, and re-layouts  5.83 us (3%)
  other arithmetic  2.17 us (1%)
    pallas_call x1, Pallas kernels, chain_local(): pl.pallas_call(layer_kernel, out_shape=(jax.ShapeDtypeStruct((count, widt...  165 us
    unnamed x8, local copies, waits for them, and re-layouts  5.83 us

profile of v3, /device:TPU:0, one launch (start us, length us, event | category | flops | bytes accessed | tf_op | source)
XLA Modules:
  0.0 173.5 jit_solution(8304229381388550580)
XLA Ops:
  0.6 0.8 compare_select_fusion
  1.4 1.4 select_reduce_fusion.weights
  2.8 164.9 %shard_map.111 = (bf16[128,2048]{1,0:T(8,128)(2,1)}, bf16[512,768]{1,0:T(8,128)(2,1)}, bf16[512,768]{1,0:T(8,128)(2,1)}, bf16[768,512]{1,0:T(8,128)(2,1)}) custom-call(bf16[128,2048]{1,0:T(8,128)(2,1)} %tokens.1, bf16[128,2048]{1,0:T(8,128)(2,1)} %grads.1, f32[8,128]{1,0:T(8,128)} %select_reduce_fusion.weights, bf16[2048,768]{1,0:T(8,128)(2,1)} %bitcast.8, ...), custom_call_target="tpu_custom_call" | custom-call | tf_op jit(solution)/shard_map/pallas_call | solution.py:499
  167.7 0.0 copy-start.1
  167.7 0.0 copy-start
  167.7 2.0 %copy.16 = bf16[128,2048]{1,0:T(8,128)(2,1)} copy(bf16[128,2048]{1,0:T(8,128)(2,1)} %get-tuple-element.16) | data formatting | bytes 1048576
  169.7 2.1 %copy.17 = bf16[1,512,768]{2,1,0:T(8,128)(2,1)} copy(bf16[1,512,768]{2,1,0:T(8,128)(2,1)} %bitcast.13) | data formatting | bytes 1572864
  171.8 0.0 copy-done.1
  171.8 0.9 copy.18
  172.7 0.0 copy-done
  172.7 0.9 copy.19
Async XLA Ops:
  167.7 4.1 %copy-start.1 = (bf16[512,768]{1,0:T(8,128)(2,1)S(1)}, bf16[512,768]{1,0:T(8,128)(2,1)}, u32[]{:S(2)}) copy-start(bf16[512,768]{1,0:T(8,128)(2,1)} %get-tuple-element.10) | copy-start | bytes 2359300
  167.7 5.0 %copy-start = (bf16[768,512]{1,0:T(8,128)(2,1)S(1)}, bf16[768,512]{1,0:T(8,128)(2,1)}, u32[]{:S(2)}) copy-start(bf16[768,512]{1,0:T(8,128)(2,1)} %get-tuple-element.11) | copy-start | bytes 2359300

commit v4 on v3

--- a/solution.py
+++ b/solution.py
@@ -184,7 +184,7 @@
         )
 
     def each_target(fn):
-        for q in range(1, chips):
+        for q in (2, 1) + tuple(range(3, chips)):
             if q < last:
                 fn(q)
             else:

time: 174 us -> 173 us (level)
  no operation moved by 1% of the time
where the time goes in v4:
time: 173 us
  Pallas kernels  164 us (95%)
  local copies, waits for them, and re-layouts  5.83 us (3%)
  other arithmetic  2.17 us (1%)
    pallas_call x1, Pallas kernels, chain_local(): pl.pallas_call(layer_kernel, out_shape=(jax.ShapeDtypeStruct((count, widt...  164 us
    unnamed x8, local copies, waits for them, and re-layouts  5.83 us

profile of v4, /device:TPU:0, one launch (start us, length us, event | category | flops | bytes accessed | tf_op | source)
XLA Modules:
  0.0 172.9 jit_solution(15445759902657052885)
XLA Ops:
  0.6 0.8 compare_select_fusion
  1.4 1.4 select_reduce_fusion.weights
  2.8 164.2 %shard_map.111 = (bf16[128,2048]{1,0:T(8,128)(2,1)}, bf16[512,768]{1,0:T(8,128)(2,1)}, bf16[512,768]{1,0:T(8,128)(2,1)}, bf16[768,512]{1,0:T(8,128)(2,1)}) custom-call(bf16[128,2048]{1,0:T(8,128)(2,1)} %tokens.1, bf16[128,2048]{1,0:T(8,128)(2,1)} %grads.1, f32[8,128]{1,0:T(8,128)} %select_reduce_fusion.weights, bf16[2048,768]{1,0:T(8,128)(2,1)} %bitcast.8, ...), custom_call_target="tpu_custom_call" | custom-call | tf_op jit(solution)/shard_map/pallas_call | solution.py:499
  167.0 0.0 copy-start.1
  167.0 0.0 copy-start
  167.0 2.0 %copy.16 = bf16[128,2048]{1,0:T(8,128)(2,1)} copy(bf16[128,2048]{1,0:T(8,128)(2,1)} %get-tuple-element.16) | data formatting | bytes 1048576
  169.0 2.1 %copy.17 = bf16[1,512,768]{2,1,0:T(8,128)(2,1)} copy(bf16[1,512,768]{2,1,0:T(8,128)(2,1)} %bitcast.13) | data formatting | bytes 1572864
  171.1 0.0 copy-done.1
  171.1 0.9 copy.18
  172.0 0.0 copy-done
  172.0 0.9 copy.19
Async XLA Ops:
  167.0 4.1 %copy-start.1 = (bf16[512,768]{1,0:T(8,128)(2,1)S(1)}, bf16[512,768]{1,0:T(8,128)(2,1)}, u32[]{:S(2)}) copy-start(bf16[512,768]{1,0:T(8,128)(2,1)} %get-tuple-element.10) | copy-start | bytes 2359300
  167.0 5.0 %copy-start = (bf16[768,512]{1,0:T(8,128)(2,1)S(1)}, bf16[768,512]{1,0:T(8,128)(2,1)}, u32[]{:S(2)}) copy-start(bf16[768,512]{1,0:T(8,128)(2,1)} %get-tuple-element.11) | copy-start | bytes 2359300
